TPU v7x, 32 devices: a whole 2x2x4 slice. The times are simulated.
32 devices in a mesh: tab: 4 (over y, x), blk: 8 (over z, core).
Axes of the slice: x: 2, y: 2, z: 4, core: 2. Of those that a mesh axis runs over, the one named last changes fastest.
Arguments:
- tokens: bfloat16 [8, 2048, 768], P('tab', 'blk'), may hold values from -6 to 6
- lengths: int32 [8], P('tab'), may hold values from 128 to 2048, as said below
- qkv_weight: bfloat16 [768, 2304], replicated, may hold values from -0.21875 to 0.21875
- qkv_bias: bfloat16 [1536], replicated, may hold values from -1 to 1
- out_weight: bfloat16 [768, 768], replicated, may hold values from -0.75 to 0.75
- out_bias: bfloat16 [768], replicated, may hold values from -3 to 3
- attn_gain: bfloat16 [768], replicated, may hold values from 0.5 to 1.5
- attn_shift: bfloat16 [768], replicated, may hold values from -3 to 3
- up_weight: bfloat16 [768, 3072], replicated, may hold values from -0.21875 to 0.21875
- up_bias: bfloat16 [3072], replicated, may hold values from -3 to 3
- down_weight: bfloat16 [3072, 768], replicated, may hold values from -0.109375 to 0.109375
- down_bias: bfloat16 [768], replicated, may hold values from -3 to 3
- ffn_gain: bfloat16 [768], replicated, may hold values from 0.5 to 1.5
- ffn_shift: bfloat16 [768], replicated, may hold values from -3 to 3
- cotangent: bfloat16 [8, 2048, 768], P('tab', 'blk'), may hold values from -6 to 6
Outputs:
- layer_out: bfloat16 [8, 2048, 768], P('tab', 'blk')
- token_grad: bfloat16 [8, 2048, 768], P('tab', 'blk')
- wgrad_qkv: float32 [768, 2304], P(('tab', 'blk'))
- bgrad_qkv: float32 [1536], P(('tab', 'blk'))
- wgrad_out: float32 [768, 768], P(('tab', 'blk'))
- bgrad_out: float32 [768], P(('tab', 'blk'))
- ggrad_attn: float32 [768], P(('tab', 'blk'))
- sgrad_attn: float32 [768], P(('tab', 'blk'))
- wgrad_up: float32 [768, 3072], P(('tab', 'blk'))
- bgrad_up: float32 [3072], P(('tab', 'blk'))
- wgrad_down: float32 [3072, 768], P(('tab', 'blk'))
- bgrad_down: float32 [768], P(('tab', 'blk'))
- ggrad_ffn: float32 [768], P(('tab', 'blk'))
- sgrad_ffn: float32 [768], P(('tab', 'blk'))
Inputs may be any that keep to these rules, and one draw needn't show every extreme that they name: `lengths`: among each 2 consecutive tables one, drawn from the seed, has exactly 2048 tokens.
All inputs are finite; a program needn't handle non-finite values.
Results may differ from a plain program's by a relative error of at most 0.023.
Values may be sent and summed in bfloat16 or wider, within the bound.
A program may use at most 192 MiB of HBM per device.

v0:
```python
import functools
import math

import jax
import jax.numpy as jnp
from jax import lax
from jax.experimental import pallas as pl
from jax.experimental.pallas import tpu as pltpu
from jax.sharding import PartitionSpec as P

HD = 64


EPSILON = 1e-05
NEGATIVE = -1e30


def from_behind(block, axis, distance):
    devices = range(lax.axis_size(axis))
    route = [((i - distance) % len(devices), i) for i in devices]
    return lax.ppermute(block, axis, route)


def norm_rows(inputs, gains, shifts):
    row_mean = jnp.mean(inputs, axis=-1, keepdims=True)
    centred = inputs - row_mean
    row_var = jnp.mean(centred * centred, axis=-1, keepdims=True)
    return centred * lax.rsqrt(row_var + EPSILON) * gains + shifts


def gelu_exact(inputs):
    return jax.nn.gelu(inputs, approximate=False)


def times_back(left, right):
    return lax.dot_general(
        left, right, (((1,), (1,)), ((), ())), preferred_element_type=jnp.float32
    )


def over_rows(left, right):
    return lax.dot_general(
        left, right, (((0,), (0,)), ((), ())), preferred_element_type=jnp.float32
    )


def shards_ring(
    tokens,
    lengths,
    qkv_weight,
    qkv_bias,
    out_weight,
    out_bias,
    attn_gain,
    attn_shift,
    up_weight,
    up_bias,
    down_weight,
    down_bias,
    ffn_gain,
    ffn_shift,
    cotangent,
):
    table_count, row_count, model_width = tokens.shape
    head_count = model_width // HD
    cycle_size = lax.axis_size("blk")
    cycle_place = lax.axis_index("blk")
    score_scale = HD ** (-0.5)
    flat_tokens = tokens.reshape(table_count * row_count, model_width)
    bias_full = jnp.concatenate(
        [
            qkv_bias[:model_width].astype(jnp.float32),
            jnp.zeros((model_width,), jnp.float32),
            qkv_bias[model_width:].astype(jnp.float32),
        ]
    )
    qkv_low = (
        jnp.dot(flat_tokens, qkv_weight, preferred_element_type=jnp.float32) + bias_full
    ).astype(jnp.bfloat16)
    queries = qkv_low[:, :model_width].reshape(table_count, row_count, head_count, HD)
    key_values = qkv_low[:, model_width:].reshape(table_count, row_count, 2 * model_width)

    def key_mask(first_row, key_count):
        positions = first_row + jnp.arange(key_count, dtype=jnp.int32)
        return (positions[None, :] < lengths[:, None])[:, None, None, :]

    def split_pair(pair_block):
        key_count = pair_block.shape[1]
        keys_part = pair_block[:, :, :model_width].reshape(table_count, key_count, head_count, HD)
        values_part = pair_block[:, :, model_width:].reshape(table_count, key_count, head_count, HD)
        return (keys_part, values_part)

    pair_block = lax.all_gather(key_values, "blk", axis=1, tiled=True)
    running_max = jnp.full((table_count, row_count, head_count), NEGATIVE, jnp.float32)
    keys_part, values_part = split_pair(pair_block)
    is_valid = key_mask(jnp.int32(0), pair_block.shape[1])
    raw_scores = jnp.einsum(
        "trhd,tkhd->trhk", queries, keys_part, preferred_element_type=jnp.float32
    )
    scores = jnp.where(is_valid, raw_scores * score_scale, NEGATIVE)
    peak_new = jnp.maximum(running_max, jnp.max(scores, axis=-1))
    exponent = jnp.where(is_valid, jnp.exp(scores - peak_new[..., None]), 0.0)
    running_sum = jnp.sum(exponent, axis=-1)
    weighted = jnp.einsum(
        "trhk,tkhd->trhd",
        exponent.astype(jnp.bfloat16),
        values_part,
        preferred_element_type=jnp.float32,
    )
    running_max, running_sum, weighted = (peak_new, running_sum, weighted)
    context = weighted / running_sum[..., None]
    log_total = running_max + jnp.log(running_sum)
    context_low = context.reshape(table_count * row_count, model_width).astype(jnp.bfloat16)
    attended = jnp.dot(
        context_low, out_weight, preferred_element_type=jnp.float32
    ) + out_bias.astype(jnp.float32)
    pre_one = flat_tokens.astype(jnp.float32) + attended
    gain_one = attn_gain.astype(jnp.float32)
    shift_one = attn_shift.astype(jnp.float32)
    hidden = norm_rows(pre_one, gain_one, shift_one)
    hidden_low = hidden.astype(jnp.bfloat16)
    upper = jnp.dot(hidden_low, up_weight, preferred_element_type=jnp.float32) + up_bias.astype(
        jnp.float32
    )
    active = gelu_exact(upper).astype(jnp.bfloat16)
    pre_two = (
        hidden
        + jnp.dot(active, down_weight, preferred_element_type=jnp.float32)
        + down_bias.astype(jnp.float32)
    )
    gain_two = ffn_gain.astype(jnp.float32)
    shift_two = ffn_shift.astype(jnp.float32)
    layer_out = norm_rows(pre_two, gain_two, shift_two).astype(jnp.bfloat16).reshape(tokens.shape)
    grad_out = cotangent.reshape(table_count * row_count, model_width).astype(jnp.float32)
    _, norm_two_back = jax.vjp(norm_rows, pre_two, gain_two, shift_two)
    grad_pre_two, ggrad_ffn, sgrad_ffn = norm_two_back(grad_out)
    grad_branch = grad_pre_two.astype(jnp.bfloat16)
    wgrad_down = over_rows(active, grad_branch)
    bgrad_down = jnp.sum(grad_branch, axis=0, dtype=jnp.float32)
    grad_active = times_back(grad_branch, down_weight)
    _, gelu_back = jax.vjp(gelu_exact, upper)
    grad_upper = gelu_back(grad_active)[0].astype(jnp.bfloat16)
    wgrad_up = over_rows(hidden_low, grad_upper)
    bgrad_up = jnp.sum(grad_upper, axis=0, dtype=jnp.float32)
    grad_hidden = grad_pre_two + times_back(grad_upper, up_weight)
    _, norm_one_back = jax.vjp(norm_rows, pre_one, gain_one, shift_one)
    grad_pre_one, ggrad_attn, sgrad_attn = norm_one_back(grad_hidden)
    grad_attended = grad_pre_one.astype(jnp.bfloat16)
    wgrad_out = over_rows(context_low, grad_attended)
    bgrad_out = jnp.sum(grad_attended, axis=0, dtype=jnp.float32)
    grad_context = times_back(grad_attended, out_weight).astype(jnp.bfloat16)
    grad_heads = grad_context.reshape(table_count, row_count, head_count, HD)
    row_delta = jnp.sum(grad_heads.astype(jnp.float32) * context, axis=-1)

    def cycle_turn_step(cycle_turn, cycle_state):
        pair_now, pair_grads, grad_queries = cycle_state
        owner_index = (cycle_place - cycle_turn) % cycle_size
        keys_part, values_part = split_pair(pair_now)
        is_valid = key_mask(owner_index * row_count, row_count)
        raw_scores = jnp.einsum(
            "trhd,tkhd->trhk", queries, keys_part, preferred_element_type=jnp.float32
        )
        scores = jnp.where(is_valid, raw_scores * score_scale, NEGATIVE)
        probs = jnp.where(is_valid, jnp.exp(scores - log_total[..., None]), 0.0)
        grad_probs = jnp.einsum(
            "trhd,tkhd->trhk", grad_heads, values_part, preferred_element_type=jnp.float32
        )
        grad_raw = (probs * (grad_probs - row_delta[..., None]) * score_scale).astype(jnp.bfloat16)
        grad_queries = grad_queries + jnp.einsum(
            "trhk,tkhd->trhd", grad_raw, keys_part, preferred_element_type=jnp.float32
        )
        grad_keys = jnp.einsum(
            "trhk,trhd->tkhd", grad_raw, queries, preferred_element_type=jnp.float32
        )
        grad_values = jnp.einsum(
            "trhk,trhd->tkhd",
            probs.astype(jnp.bfloat16),
            grad_heads,
            preferred_element_type=jnp.float32,
        )
        pair_grads = pair_grads + jnp.concatenate(
            [
                grad_keys.reshape(table_count, row_count, model_width),
                grad_values.reshape(table_count, row_count, model_width),
            ],
            axis=-1,
        )
        pair_next = from_behind(pair_now, "blk", 1)
        grads_next = from_behind(pair_grads.astype(jnp.bfloat16), "blk", 1).astype(pair_grads.dtype)
        return (pair_next, grads_next, grad_queries)

    cycle_start = (
        key_values,
        jnp.zeros((table_count, row_count, 2 * model_width), jnp.float32),
        jnp.zeros((table_count, row_count, head_count, HD), jnp.float32),
    )
    _, pair_home, grad_queries = lax.fori_loop(0, cycle_size, cycle_turn_step, cycle_start)
    grad_qkv = jnp.concatenate(
        [
            grad_queries.reshape(table_count * row_count, model_width),
            pair_home.reshape(table_count * row_count, 2 * model_width),
        ],
        axis=-1,
    ).astype(jnp.bfloat16)
    wgrad_qkv = over_rows(flat_tokens, grad_qkv)
    column_sums = jnp.sum(grad_qkv, axis=0, dtype=jnp.float32)
    bgrad_qkv = jnp.concatenate([column_sums[:model_width], column_sums[2 * model_width :]])
    token_grad = (
        (grad_pre_one + times_back(grad_qkv, qkv_weight)).astype(jnp.bfloat16).reshape(tokens.shape)
    )
    (
        wgrad_qkv,
        bgrad_qkv,
        wgrad_out,
        bgrad_out,
        ggrad_attn,
        sgrad_attn,
        wgrad_up,
        bgrad_up,
        wgrad_down,
        bgrad_down,
        ggrad_ffn,
        sgrad_ffn,
    ) = (
        lax.psum_scatter(
            wgrad_qkv.astype(jnp.bfloat16), "tab", scatter_dimension=0, tiled=True
        ).astype(jnp.float32),
        lax.psum_scatter(
            bgrad_qkv.astype(jnp.bfloat16), "tab", scatter_dimension=0, tiled=True
        ).astype(jnp.float32),
        lax.psum_scatter(
            wgrad_out.astype(jnp.bfloat16), "tab", scatter_dimension=0, tiled=True
        ).astype(jnp.float32),
        lax.psum_scatter(
            bgrad_out.astype(jnp.bfloat16), "tab", scatter_dimension=0, tiled=True
        ).astype(jnp.float32),
        lax.psum_scatter(
            ggrad_attn.astype(jnp.bfloat16), "tab", scatter_dimension=0, tiled=True
        ).astype(jnp.float32),
        lax.psum_scatter(
            sgrad_attn.astype(jnp.bfloat16), "tab", scatter_dimension=0, tiled=True
        ).astype(jnp.float32),
        lax.psum_scatter(
            wgrad_up.astype(jnp.bfloat16), "tab", scatter_dimension=0, tiled=True
        ).astype(jnp.float32),
        lax.psum_scatter(
            bgrad_up.astype(jnp.bfloat16), "tab", scatter_dimension=0, tiled=True
        ).astype(jnp.float32),
        lax.psum_scatter(
            wgrad_down.astype(jnp.bfloat16), "tab", scatter_dimension=0, tiled=True
        ).astype(jnp.float32),
        lax.psum_scatter(
            bgrad_down.astype(jnp.bfloat16), "tab", scatter_dimension=0, tiled=True
        ).astype(jnp.float32),
        lax.psum_scatter(
            ggrad_ffn.astype(jnp.bfloat16), "tab", scatter_dimension=0, tiled=True
        ).astype(jnp.float32),
        lax.psum_scatter(
            sgrad_ffn.astype(jnp.bfloat16), "tab", scatter_dimension=0, tiled=True
        ).astype(jnp.float32),
    )
    (
        wgrad_qkv,
        bgrad_qkv,
        wgrad_out,
        bgrad_out,
        ggrad_attn,
        sgrad_attn,
        wgrad_up,
        bgrad_up,
        wgrad_down,
        bgrad_down,
        ggrad_ffn,
        sgrad_ffn,
    ) = (
        lax.psum_scatter(
            wgrad_qkv.astype(jnp.bfloat16), "blk", scatter_dimension=0, tiled=True
        ).astype(jnp.float32),
        lax.psum_scatter(
            bgrad_qkv.astype(jnp.bfloat16), "blk", scatter_dimension=0, tiled=True
        ).astype(jnp.float32),
        lax.psum_scatter(
            wgrad_out.astype(jnp.bfloat16), "blk", scatter_dimension=0, tiled=True
        ).astype(jnp.float32),
        lax.psum_scatter(
            bgrad_out.astype(jnp.bfloat16), "blk", scatter_dimension=0, tiled=True
        ).astype(jnp.float32),
        lax.psum_scatter(
            ggrad_attn.astype(jnp.bfloat16), "blk", scatter_dimension=0, tiled=True
        ).astype(jnp.float32),
        lax.psum_scatter(
            sgrad_attn.astype(jnp.bfloat16), "blk", scatter_dimension=0, tiled=True
        ).astype(jnp.float32),
        lax.psum_scatter(
            wgrad_up.astype(jnp.bfloat16), "blk", scatter_dimension=0, tiled=True
        ).astype(jnp.float32),
        lax.psum_scatter(
            bgrad_up.astype(jnp.bfloat16), "blk", scatter_dimension=0, tiled=True
        ).astype(jnp.float32),
        lax.psum_scatter(
            wgrad_down.astype(jnp.bfloat16), "blk", scatter_dimension=0, tiled=True
        ).astype(jnp.float32),
        lax.psum_scatter(
            bgrad_down.astype(jnp.bfloat16), "blk", scatter_dimension=0, tiled=True
        ).astype(jnp.float32),
        lax.psum_scatter(
            ggrad_ffn.astype(jnp.bfloat16), "blk", scatter_dimension=0, tiled=True
        ).astype(jnp.float32),
        lax.psum_scatter(
            sgrad_ffn.astype(jnp.bfloat16), "blk", scatter_dimension=0, tiled=True
        ).astype(jnp.float32),
    )
    return (
        layer_out,
        token_grad,
        wgrad_qkv,
        bgrad_qkv,
        wgrad_out,
        bgrad_out,
        ggrad_attn,
        sgrad_attn,
        wgrad_up,
        bgrad_up,
        wgrad_down,
        bgrad_down,
        ggrad_ffn,
        sgrad_ffn,
    )


GROUPS = 4
LANES = 128
LOG2E = math.log2(math.e)
MESH = pl.DeviceIdType.MESH


def times_t(left, right):
    return lax.dot_general(
        left, right, (((1,), (1,)), ((), ())), preferred_element_type=jnp.float32
    )


def place():
    tab, blk = lax.axis_index("tab"), lax.axis_index("blk")
    return tab, blk, blk // 2, blk % 2


def meet(tab, blk):
    barrier = pltpu.get_barrier_semaphore()

    @pl.loop(1, 8)
    def _(step):
        pl.semaphore_signal(
            barrier, inc=1, device_id=(tab, lax.rem(blk + step, 8)), device_id_type=MESH
        )

    pl.semaphore_wait(barrier, 7)


def greet_all(tab, blk):
    barrier = pltpu.get_barrier_semaphore()
    for step in range(1, 8):
        pl.semaphore_signal(
            barrier, inc=1, device_id=(tab, lax.rem(blk + step, 8)), device_id_type=MESH
        )
    for step in range(1, 4):
        pl.semaphore_signal(
            barrier, inc=1, device_id=(lax.rem(tab + step, 4), blk), device_id_type=MESH
        )
    pl.semaphore_wait(barrier, 10)


def send_to(src, dst, send_sem, recv_sem, device):
    return pltpu.make_async_remote_copy(
        src_ref=src,
        dst_ref=dst,
        send_sem=send_sem,
        recv_sem=recv_sem,
        device_id=device,
        device_id_type=MESH,
    )


def landed(ref, sem):
    pltpu.make_async_copy(ref, ref, sem).wait()


def return_rows(src, dst, send_sem, recv_sem, act):
    tab, _, chip, core = place()
    half, group = chip // 2, 2 * lax.rem(chip, 2) + core
    for side in range(2):
        is_own = jnp.logical_and(chip == group, core == side)
        own = pltpu.make_async_copy(src.at[side], dst.at[half], recv_sem.at[half])
        away = send_to(
            src.at[side],
            dst.at[half],
            send_sem.at[side],
            recv_sem.at[half],
            (tab, 2 * group + side),
        )
        if act == "start":
            pl.when(is_own)(own.start)
            pl.when(jnp.logical_not(is_own))(away.start)
        else:
            pl.when(jnp.logical_not(is_own))(away.wait_send)
            landed(dst.at[side], recv_sem.at[side])


def by_core(core, act):
    pl.when(core == 0)(functools.partial(act, 0))
    pl.when(core == 1)(functools.partial(act, 1))


def fold(block):
    cut = block.shape[0] // 2
    return jnp.concatenate([block[:cut], block[cut:]], axis=1)


def unfold(block):
    cut = block.shape[1] // 2
    return jnp.concatenate([block[:, :cut], block[:, cut:]], axis=0)


def own_window(group, first, rows_ref, out):
    start = pl.multiple_of(first + LANES * ((3 * group) // 2), LANES)
    window = rows_ref[:, pl.ds(start, 2 * LANES)].astype(jnp.float32)
    window = pltpu.roll(window, lax.rem(2 * LANES - HD * lax.rem(group, 2), 2 * LANES), 1)
    left = window[:, :LANES]
    low = lax.broadcasted_iota(jnp.int32, left.shape, 1) < HD
    for head, lanes in enumerate((left, pltpu.roll(left, HD, 1), window[:, LANES:])):
        out(head, jnp.where(low, lanes, 0.0))


def attend_kernel(
    heads,
    tok_ref,
    len_ref,
    par_ref,
    w_hbm,
    cot_hbm,
    ctx_ref,
    mytok_ref,
    mycot_ref,
    fullt_ref,
    qkv_ref,
    ot_ref,
    lse_ref,
    wr_ref,
    tokv,
    toktv,
    wfull,
    wrv,
    wown,
    bown,
    qkvv,
    vtv,
    otv,
    lsev,
    acc,
    peaks,
    csend,
    send_sem,
    recv,
    csend_sem,
    crecv_sem,
    osend_sem,
    orecv_sem,
    local_sem,
):
    tab, blk, chip, core = place()
    half = chip // 2
    group = 2 * lax.rem(chip, 2) + core
    rows = tok_ref.shape[1]
    width = tok_ref.shape[2]
    is_near = jnp.logical_or(chip == 1, chip == 2)
    mate = chip + 1 - 2 * lax.rem(chip, 2)
    other_near = 2 - half
    other_far = 3 - 3 * half
    own_far = 3 * half
    scale = LOG2E / math.sqrt(HD)

    def remote(src, dst, send_sem, recv_sem, to_chip, to_core):
        return pltpu.make_async_remote_copy(
            src_ref=src,
            dst_ref=dst,
            send_sem=send_sem,
            recv_sem=recv_sem,
            device_id=(tab, 2 * to_chip + to_core),
            device_id_type=MESH,
        )

    here, there = tok_ref.at[half], tok_ref.at[1 - half]
    to_mate = remote(here, tokv.at[blk], send_sem.at[0], recv.at[blk], mate, core)
    to_other = remote(there, tokv.at[blk], send_sem.at[1], recv.at[blk], other_near, core)
    to_side = remote(here, tokv.at[blk], send_sem.at[2], recv.at[blk], chip, 1 - core)

    def to_far(slot, src_chip):
        which = 2 * src_chip + core
        ref = tokv.at[which]
        return remote(ref, ref, send_sem.at[2 + slot], recv.at[which], own_far, core)

    def to_core(slot, src_chip):
        which = 2 * src_chip + core
        ref = tokv.at[which]
        return remote(ref, ref, send_sem.at[5 + slot], recv.at[which], chip, 1 - core)

    def arrived(which):
        pltpu.make_async_copy(tokv.at[which], tokv.at[which], recv.at[which]).wait()

    load = pltpu.make_async_copy(w_hbm, wfull, local_sem.at[5])
    load.start()
    meet(tab, blk)
    pl.when(is_near)(to_other.start)
    to_mate.start()
    to_side.start()
    tokv[blk] = tok_ref[half]

    lane1 = lax.broadcasted_iota(jnp.int32, (8, LANES), 1)
    for at in (0, 2):

        def keep_bias(head, lanes, at=at):
            row = jnp.where(lane1 == HD, 1.0, lanes)
            bown[:, pl.ds((at * heads + head) * LANES, LANES)] = row

        own_window(group, 0, par_ref.at[pl.ds(8 * (1 + at // 2), 8)], keep_bias)
    for head in range(heads):
        bown[:, pl.ds((heads + head) * LANES, LANES)] = jnp.zeros((8, LANES), jnp.float32)
    load.wait()
    for at in range(3):

        def keep_weight(head, lanes, at=at):
            wown[:, pl.ds((at * heads + head) * LANES, LANES)] = lanes.astype(jnp.bfloat16)

        own_window(group, at * width, wfull, keep_weight)

    length = len_ref[half]
    lane = lax.broadcasted_iota(jnp.int32, (rows, LANES), 1)
    row = lax.broadcasted_iota(jnp.int32, (rows, LANES), 0)

    def project(which):
        first = pl.multiple_of(which * rows, rows)
        tok = tokv[which]
        y = jnp.dot(tok, wown[...], preferred_element_type=jnp.float32) + bown[:1]
        pad = jnp.where((lane == HD) & (row + first >= length), NEGATIVE, 0.0)
        for head in range(heads):
            q, k, v = (
                y[:, (part * heads + head) * LANES :][:, :LANES] for part in range(3)
            )
            qkvv[head, pl.ds(first, rows)] = q.astype(jnp.bfloat16)
            qkvv[heads + head, pl.ds(first, rows)] = (k + pad).astype(jnp.bfloat16)
            qkvv[2 * heads + head, pl.ds(first, rows)] = v.astype(jnp.bfloat16)
            vtv[head, :, pl.ds(first, rows)] = v.T.astype(jnp.bfloat16)
        toktv[:, pl.ds(first, rows)] = tok.T

    def take_keys(tile, head, first_key, count, fresh):
        queries = pl.ds(pl.multiple_of(tile * 2 * rows, 2 * rows), 2 * rows)
        keys = pl.ds(pl.multiple_of(first_key, count), count)
        st = times_t(qkvv[heads + head, keys], qkvv[head, queries])
        peak = jnp.max(st, axis=0, keepdims=True)
        if not fresh:
            before = peaks[tile, pl.ds(head, 1)]
            peak = jnp.maximum(peak, before)
        pt = jnp.exp2((st - peak) * scale).astype(jnp.bfloat16)
        ot = jnp.dot(vtv[head, :, keys], pt, preferred_element_type=jnp.float32)
        if not fresh:
            ot += acc[tile, head] * jnp.exp2((before - peak) * scale)
        acc[tile, head] = ot
        peaks[tile, pl.ds(head, 1)] = peak

    def meet_keys_of_own_half():
        @pl.loop(0, 2 * heads)
        def _(at):
            tile = jnp.where(at < heads, chip, mate)
            take_keys(tile, lax.rem(at, heads), half * 4 * rows, 4 * rows, True)

    def meet_keys_of_near():
        @pl.loop(0, heads)
        def _(head):
            take_keys(other_near, head, half * 4 * rows, 4 * rows, True)

        @pl.loop(0, 3 * heads)
        def _(at):
            tile = jnp.where(at < heads, chip, jnp.where(at < 2 * heads, mate, other_near))
            take_keys(tile, lax.rem(at, heads), other_near * 2 * rows, 2 * rows, False)

    project(blk)

    def half_lanes(part, at):
        first = part * width + LANES * (at // 2)
        return wfull[:, first : first + LANES][:, HD * (at % 2) :][:, :HD]

    for head in range(heads):
        for part in range(3):
            for pair in range(GROUPS // 2):
                at = 2 * pair * heads + head
                wrv[head, :, pl.ds((2 * part + pair) * LANES, LANES)] = jnp.concatenate(
                    [half_lanes(part, at), half_lanes(part, at + heads)], axis=1
                )
    arrived(2 * mate + core)
    to_core(0, mate).start()

    @pl.when(jnp.logical_not(is_near))
    def _():
        to_mate.wait_send()
        to_other.start()

    project(2 * mate + core)
    arrived(2 * chip + 1 - core)
    project(2 * chip + 1 - core)
    arrived(2 * mate + 1 - core)
    project(2 * mate + 1 - core)

    def pass_on(slot, src_chip):
        arrived(2 * src_chip + core)
        pl.when(is_near)(to_far(slot, src_chip).start)
        to_core(slot, src_chip).start()

    def project_chip(src_chip):
        project(2 * src_chip + core)
        arrived(2 * src_chip + 1 - core)
        project(2 * src_chip + 1 - core)

    def owner_of(table):
        return 2 * table + chip // 2, lax.rem(chip, 2)

    def cotangent_copy(table, own):
        src, dst = cot_hbm.at[table], mycot_ref.at[core]
        if own:
            return pltpu.make_async_copy(src, dst, orecv_sem.at[core])
        return remote(src, dst, osend_sem.at[table], orecv_sem.at[core], *owner_of(table))

    def is_owner(table):
        to_chip, to_core = owner_of(table)
        return jnp.logical_and(to_chip == chip, to_core == core)

    pl.when(is_near)(functools.partial(pass_on, 1, other_near))
    meet_keys_of_own_half()
    pl.when(jnp.logical_not(is_near))(functools.partial(pass_on, 1, other_near))
    pl.when(is_near)(functools.partial(pass_on, 2, other_far))
    cotangent_copy(1 - half, False).start()
    project_chip(other_near)
    meet_keys_of_near()
    pl.when(jnp.logical_not(is_near))(functools.partial(pass_on, 2, other_far))
    project_chip(other_far)

    keep = (
        pltpu.make_async_copy(toktv, fullt_ref, local_sem.at[0]),
        pltpu.make_async_copy(qkvv, qkv_ref, local_sem.at[1]),
        pltpu.make_async_copy(wrv, wr_ref, local_sem.at[6]),
    )
    for copy in keep:
        copy.start()

    pl.when(is_owner(half))(cotangent_copy(half, True).start)
    pl.when(jnp.logical_not(is_owner(half)))(cotangent_copy(half, False).start)
    my_tokens = [
        pltpu.make_async_copy(
            tokv.at[2 * group + side], mytok_ref.at[side], local_sem.at[7 + side]
        )
        for side in range(2)
    ]
    for copy in my_tokens:
        copy.start()

    def context_copy(which):
        return remote(
            csend.at[which],
            ctx_ref.at[group],
            csend_sem.at[which],
            crecv_sem.at[group],
            2 * half + which // 2,
            lax.rem(which, 2),
        )

    own_context = pltpu.make_async_copy(
        csend.at[group], ctx_ref.at[group], local_sem.at[2]
    )

    @pl.loop(0, 4)
    def _(step):
        at = jnp.where(is_near, step, 3 - step)
        which = jnp.where(
            at < 2, jnp.where(at == 0, chip, mate), jnp.where(at == 2, other_near, other_far)
        )

        @pl.when(at == 3)
        def _():
            @pl.loop(0, heads)
            def _(head):
                take_keys(which, head, 0, 8 * rows, True)

        @pl.when(at < 3)
        def _():
            @pl.loop(0, heads)
            def _(head):
                take_keys(which, head, other_far * 2 * rows, 2 * rows, False)

        for head in range(heads):
            ot = acc[which, head]
            total = ot[HD : HD + 1]
            otv[which, head * HD : (head + 1) * HD] = ot[:HD] / total
            peak = peaks[which, head : head + 1]
            lsev[which, head : head + 1] = peak * scale + jnp.log(total) * LOG2E
        csend[which] = fold(otv[which].T.astype(jnp.bfloat16))

        pl.when(which == group)(own_context.start)
        pl.when(which != group)(context_copy(which).start)

    more = (
        pltpu.make_async_copy(otv, ot_ref, local_sem.at[3]),
        pltpu.make_async_copy(lsev, lse_ref, local_sem.at[4]),
    )
    for copy in more:
        copy.start()
    pl.when(is_near)(to_mate.wait_send)
    to_other.wait_send()
    to_side.wait_send()
    to_core(0, mate).wait_send()
    for slot, src_chip in ((1, other_near), (2, other_far)):
        pl.when(is_near)(to_far(slot, src_chip).wait_send)
        to_core(slot, src_chip).wait_send()

    for step in range(1, 4):
        which = lax.rem(group + step, 4)
        context_copy(which).wait_send()
        pltpu.make_async_copy(ctx_ref.at[which], ctx_ref.at[which], crecv_sem.at[which]).wait()
    own_context.wait()
    pl.when(jnp.logical_not(is_owner(half)))(cotangent_copy(half, False).wait_send)
    cotangent_copy(1 - half, False).wait_send()
    for side in range(2):
        pltpu.make_async_copy(mycot_ref.at[side], mycot_ref.at[side], orecv_sem.at[side]).wait()
    for copy in [*keep, *more, *my_tokens]:
        copy.wait()


def attend(tokens, lengths, params, qkv_weight, cotangent, heads):
    _, rows, width = tokens.shape
    blocks = 8
    total = blocks * rows
    any_space = pl.BlockSpec(memory_space=pl.ANY)
    vmem = pl.BlockSpec(memory_space=pltpu.VMEM)
    bf16, f32 = jnp.bfloat16, jnp.float32
    dma = pltpu.SemaphoreType.DMA
    return pl.pallas_call(
        functools.partial(attend_kernel, heads),
        name="attend",
        out_shape=(
            jax.ShapeDtypeStruct((GROUPS, rows, 2 * heads * HD), bf16),
            jax.ShapeDtypeStruct((2, rows, width), bf16),
            jax.ShapeDtypeStruct((2, rows, width), bf16),
            jax.ShapeDtypeStruct((width, total), bf16),
            jax.ShapeDtypeStruct((3 * heads, total, LANES), bf16),
            jax.ShapeDtypeStruct((4, heads * HD, 2 * rows), f32),
            jax.ShapeDtypeStruct((4, 8, 2 * rows), f32),
            jax.ShapeDtypeStruct((heads, width, width), bf16),
        ),
        in_specs=[vmem, pl.BlockSpec(memory_space=pltpu.SMEM), vmem, any_space, any_space],
        out_specs=(any_space,) * 8,
        scratch_shapes=[
            pltpu.VMEM((blocks, rows, width), bf16),
            pltpu.VMEM((width, total), bf16),
            pltpu.VMEM(qkv_weight.shape, bf16),
            pltpu.VMEM((heads, width, width), bf16),
            pltpu.VMEM((width, 3 * heads * LANES), bf16),
            pltpu.VMEM((8, 3 * heads * LANES), f32),
            pltpu.VMEM((3 * heads, total, LANES), bf16),
            pltpu.VMEM((heads, LANES, total), bf16),
            pltpu.VMEM((4, heads * HD, 2 * rows), f32),
            pltpu.VMEM((4, 8, 2 * rows), f32),
            pltpu.VMEM((4, heads, LANES, 2 * rows), f32),
            pltpu.VMEM((4, 8, 2 * rows), f32),
            pltpu.VMEM((GROUPS, rows, 2 * heads * HD), bf16),
            dma((8,)),
            dma((blocks,)),
            dma((GROUPS,)),
            dma((GROUPS,)),
            dma((2,)),
            dma((2,)),
            dma((9,)),
        ],
        compiler_params=pltpu.CompilerParams(
            collective_id=1, has_side_effects=True, vmem_limit_bytes=60 << 20
        ),
    )(tokens, lengths, params, qkv_weight, cotangent)


UNITS = 9
TURNS = 4
STAGES = 5
PHASE = ((1, 3), (2, 5), (3, 8), (4, 11))


def attend_back_kernel(
    heads,
    dctx_ref,
    qkv_ref,
    ot_ref,
    lse_ref,
    fullt_ref,
    w_ref,
    pre_ref,
    sums_ref,
    parts_ref,
    small_ref,
    tgrad_ref,
    wqkv_ref,
    wout_ref,
    wup_ref,
    wdown_ref,
    little_ref,
    dov,
    doh,
    deltas,
    qkvv,
    otv,
    lsev,
    toktv,
    wv,
    prev,
    ktv,
    dqv,
    dkv,
    dvv,
    dqkv,
    qsend,
    kvsend,
    arrive_q,
    arrive_kv,
    joined,
    xacc,
    xsend,
    mine,
    sum0,
    sum1,
    sum2,
    sum3,
    sum4,
    slab,
    slab_in,
    sums,
    sums_in,
    line,
    line_in,
    small_in,
    small_sum,
    small_pairs,
    dsend_sem,
    drecv_sem,
    gsend_sem,
    grecv_sem,
    xsend_sem,
    xrecv_sem,
    ssend_sem,
    srecv_sem,
    tsend_sem,
    trecv_sem,
    lsend_sem,
    lrecv_sem,
    local_sem,
    mine_sem,
):
    f32, bf16 = jnp.float32, jnp.bfloat16
    tab, blk, chip, core = place()
    y, x, zh, zl = tab // 2, lax.rem(tab, 2), chip // 2, lax.rem(chip, 2)
    half = zh
    group = 2 * zl + core
    blocks, rows = 8, dov.shape[1]
    width = toktv.shape[0]
    tile = 2 * rows
    piece = 256
    scale = LOG2E / math.sqrt(HD)
    shrink = HD**-0.5

    remote = send_to

    loads = [
        pltpu.make_async_copy(src, dst, local_sem.at[at])
        for at, (src, dst) in enumerate(
            (
                (qkv_ref, qkvv),
                (ot_ref, otv),
                (lse_ref, lsev),
                (dctx_ref.at[group], dov.at[group]),
                (fullt_ref, toktv),
                (w_ref, wv),
                (pre_ref, prev),
                (sums_ref, sum0.at[: UNITS - 1]),
            )
        )
    ]
    for copy in [*loads[:4], loads[7]]:
        copy.start()

    greet_all(tab, blk)

    def group_at(step):
        to_chip = jnp.where(step < 2, zl, 1 - zl)
        return 2 * to_chip + jnp.where(lax.rem(step, 2) == 0, core, 1 - core)

    def context_copy(which):
        return remote(
            dctx_ref.at[which],
            dov.at[group],
            dsend_sem.at[which],
            drecv_sem.at[group],
            (tab, 4 * half + which),
        )

    for step in range(1, 4):
        context_copy(group_at(step)).start()

    def stage_copy(stage, unit, order=None, held=None):
        held = sum0 if held is None else held
        send, done = ssend_sem.at[stage, unit], srecv_sem.at[stage, unit]
        if stage == 0:
            src = parts_ref.at[:, :, :, :, 1 - core]
            return remote(src, sum0.at[unit], send, done, (tab, 2 * chip + 1 - core))
        if stage == 1 and order == 0:
            return remote(
                held.at[unit, :, 1 - x], sum1.at[unit], send, done, (2 * y + 1 - x, blk)
            )
        if stage == 1:
            return remote(
                held.at[unit, 1 - y], sum1.at[unit], send, done, (2 * (1 - y) + x, blk)
            )
        if stage == 2 and order == 0:
            return remote(
                sum1.at[unit, 1 - y], sum2.at[unit], send, done, (2 * (1 - y) + x, blk)
            )
        if stage == 2:
            return remote(
                sum1.at[unit, 1 - x], sum2.at[unit], send, done, (2 * y + 1 - x, blk)
            )
        if stage == 3:
            src, there = sum2.at[unit, :, 1 - zl], 2 * zh + 1 - zl
            return remote(src, sum3.at[unit], send, done, (tab, 2 * there + core))
        src, there = sum3.at[unit, 1 - zh], 2 * (1 - zh) + zl
        return remote(src, sum4.at[unit], send, done, (tab, 2 * there + core))

    both = functools.partial(by_core, core)
    mine_copy = pltpu.make_async_copy(
        parts_ref.at[:, :, :, :, core], mine, mine_sem.at[0]
    )

    def finish(unit):
        done = sum4[unit].astype(f32) + sum3[unit, zh].astype(f32)
        top, low = done[: done.shape[0] // 2], done[done.shape[0] // 2 :]
        each, cut = top.shape

        @pl.when(unit < 4)
        def _():
            at = pl.ds(pl.multiple_of(unit * each, each), each)
            wdown_ref[at, :cut] = top
            wdown_ref[at, cut:] = low

        @pl.when(jnp.logical_and(unit >= 4, unit < 8))
        def _():
            at = pl.multiple_of((unit - 4) * 2 * cut, 2 * cut)
            wup_ref[:, pl.ds(at, cut)] = top
            wup_ref[:, pl.ds(pl.multiple_of(at + cut, cut), cut)] = low

        @pl.when(unit == 8)
        def _():
            wout_ref[:, :cut] = top
            wout_ref[:, cut:] = low

    def advance(stage, unit):
        if stage == 0:
            landed(sum0.at[unit], srecv_sem.at[0, unit])
            mine_copy.wait()
            for a in range(2):
                for b in range(2):
                    sum0[unit, a, b] = sum0[unit, a, b] + mine[a, b]

            both(lambda order: stage_copy(1, unit, order).start())
        elif stage == 1:
            landed(sum1.at[unit], srecv_sem.at[1, unit])

            def act(order):
                own = sum0[unit, :, x] if order == 0 else sum0[unit, y]
                sum1[unit] = sum1[unit] + own
                stage_copy(2, unit, order).start()

            both(act)
        elif stage == 2:
            landed(sum2.at[unit], srecv_sem.at[2, unit])

            def act(order):
                sum2[unit] = sum2[unit] + sum1[unit, y if order == 0 else x]

            both(act)
            stage_copy(3, unit).start()
        elif stage == 3:
            landed(sum3.at[unit], srecv_sem.at[3, unit])
            sum3[unit] = sum3[unit] + sum2[unit, :, zl]
            stage_copy(4, unit).start()
        else:
            landed(sum4.at[unit], srecv_sem.at[4, unit])
            finish(unit)

    def tick(now):
        @pl.when(now < UNITS - 1)
        def _():
            both(lambda order: stage_copy(1, now, order, sums_ref).start())

        pl.when(now == UNITS - 1)(functools.partial(advance, 0, UNITS - 1))
        for stage, lag in PHASE:
            unit = now - lag
            due = (unit >= 0) & (unit < UNITS)
            pl.when(due)(functools.partial(advance, stage, unit))

    stage_copy(0, UNITS - 1).start()
    mine_copy.start()

    def tab_copy(src, dst, sem_at, step):
        there = lax.rem(tab + step, 4)
        return remote(
            src(there), dst(tab), tsend_sem.at[sem_at, there], trecv_sem.at[sem_at, tab], (there, blk)
        )

    def line_copy(src, dst, sem_at, step):
        there = lax.rem(blk + step, 8)
        return remote(
            src(there), dst(blk), lsend_sem.at[sem_at, there], lrecv_sem.at[sem_at, blk], (tab, there)
        )

    def small_tab(step):
        return tab_copy(lambda t: small_ref, lambda t: small_in.at[t], heads, step)

    def small_pair(at):
        there = (2 * chip + 1 - core, 2 * (2 * zh + 1 - zl) + core, 2 * (2 * (1 - zh) + zl) + core)
        return remote(
            small_sum.at[at],
            small_pairs.at[at],
            lsend_sem.at[heads, at],
            lrecv_sem.at[heads, at],
            (tab, there[at]),
        )

    def slab_tab(head, step):
        return tab_copy(
            lambda t: slab.at[head, t], lambda t: slab_in.at[head, t], head, step
        )

    def slab_blk(head, step):
        return line_copy(
            lambda b: line.at[head, b], lambda b: line_in.at[head, b], head, step
        )

    for step in range(1, 4):
        small_tab(step).start()

    def pass_small(at):
        if at == 0:
            total = small_ref[...]
            for step in range(1, 4):
                there = lax.rem(tab + step, 4)
                landed(small_in.at[there], trecv_sem.at[heads, there])
                total += small_in[there]
        else:
            landed(small_pairs.at[at - 1], lrecv_sem.at[heads, at - 1])
            total = small_sum[at - 1] + small_pairs[at - 1]
        small_sum[at] = total
        if at < 3:
            small_pair(at).start()

    def sums_tab(head, step):
        return tab_copy(
            lambda t: sums.at[head], lambda t: sums_in.at[head, t], heads + 1 + head, step
        )

    def make_slab(head):
        flat = dqkv[head]
        sums[head] = jnp.broadcast_to(
            jnp.sum(flat.astype(f32), axis=0, keepdims=True), (8, 3 * HD)
        )
        grad = jnp.dot(toktv[...], flat, preferred_element_type=f32)
        each = width // 32
        slab[head, :, :4] = grad[:, : 2 * HD].reshape(4, 4, 2 * each, 2 * HD).astype(bf16)
        q = grad[:, 2 * HD :].reshape(16, 2, each, HD)
        q = jnp.concatenate([q[:, 0], q[:, 1]], axis=2)
        slab[head, :, 4:] = q.reshape(4, 2, 2 * each, 2 * HD).astype(bf16)
        for step in range(1, 4):
            slab_tab(head, step).start()
            sums_tab(head, step).start()

    def pass_slab(head):
        total = slab[head, tab].astype(f32)
        sums_total = sums[head]
        for step in range(1, 4):
            there = lax.rem(tab + step, 4)
            landed(slab_in.at[head, there], trecv_sem.at[head, there])
            landed(sums_in.at[head, there], trecv_sem.at[heads + 1 + head, there])
            total += slab_in[head, there].astype(f32)
            sums_total += sums_in[head, there]
        each = width // 32
        for b in range(8):
            kv = total[b // 2, b % 2 * each :][:each]
            q = total[4 + b // 4, b // 2 % 2 * each :][:each, b % 2 * HD :][:, :HD]
            rows_b = jnp.concatenate([jnp.concatenate([kv, q], axis=1), sums_total], axis=0)
            line[head, b] = fold(rows_b).astype(bf16)
        line_in[head, blk] = line[head, blk]
        for step in range(1, 8):
            slab_blk(head, step).start()

    for copy in loads[:4]:
        copy.wait()
    for head in range(heads):
        ktv[head] = qkvv[heads + head].T

    def gradient_copies(head, which, own):
        slot = group * heads + head
        pairs = (
            (qsend.at[head, which], arrive_q.at[slot]),
            (kvsend.at[head, which], arrive_kv.at[slot]),
        )
        for kind, (src, dst) in enumerate(pairs):
            if own:
                yield pltpu.make_async_copy(src, dst, grecv_sem.at[kind, slot])
            else:
                yield remote(
                    src,
                    dst,
                    gsend_sem.at[kind, head, which],
                    grecv_sem.at[kind, slot],
                    (tab, 4 * half + which),
                )

    def send_gradient(kind, head, which):
        @pl.when(which == group)
        def _():
            list(gradient_copies(head, which, True))[kind].start()

        @pl.when(which != group)
        def _():
            list(gradient_copies(head, which, False))[kind].start()

    def absorb(head):
        for at in range(GROUPS):
            slot = at * heads + head
            landed(arrive_q.at[slot], grecv_sem.at[0, slot])
            landed(arrive_kv.at[slot], grecv_sem.at[1, slot])
        for pair in range(GROUPS // 2):
            left, right = 2 * pair * heads + head, (2 * pair + 1) * heads + head
            lanes = slice(pair * LANES, (pair + 1) * LANES)
            for side in range(2):
                cut = slice(side * HD, (side + 1) * HD)
                joined[side * rows : (side + 1) * rows, lanes] = jnp.concatenate(
                    [arrive_q[left][:, cut], arrive_q[right][:, cut]], axis=1
                )
                lanes_kv = slice((2 * side + 2 + pair) * LANES, (2 * side + 3 + pair) * LANES)
                joined[:, lanes_kv] = jnp.concatenate(
                    [arrive_kv[left][:, cut], arrive_kv[right][:, cut]], axis=1
                )

    @pl.loop(0, heads * TURNS)
    def _(turn):
        head, step = turn // TURNS, lax.rem(turn, TURNS)
        which = group_at(step)
        first = pl.multiple_of(which * tile, tile)

        @pl.when(head == 0)
        def _():
            @pl.when(step > 0)
            def _():
                landed(dov.at[which], drecv_sem.at[which])

            dos = unfold(dov[which])
            for at in range(heads):
                do = dos[:, at * HD : (at + 1) * HD]
                doh[at, pl.ds(first, tile)] = do
                ot = otv[which, at * HD : (at + 1) * HD]
                deltas[at, which, :1] = jnp.sum(ot * do.astype(f32).T, axis=0, keepdims=True)

        @pl.when(step == 0)
        def _():
            dkv[...] = jnp.zeros_like(dkv)
            dvv[...] = jnp.zeros_like(dvv)

        @pl.when(turn == 1)
        def _():
            for copy in loads[4:7]:
                copy.start()

        pl.when(turn == PHASE[0][1])(loads[7].wait)
        tick(turn)

        q_full = qkvv[head, pl.ds(first, tile)]
        q = q_full[:, :HD]
        do = doh[head, pl.ds(first, tile)]
        delta = deltas[head, which, :1]
        lse = lsev[which, pl.ds(head, 1)]
        dqt = jnp.zeros((LANES, tile), f32)
        for at in range(blocks * rows // piece):
            cut = pl.ds(at * piece, piece)
            st = times_t(qkvv[heads + head, cut], q_full)
            pt = jnp.exp2(st * scale - lse)
            dpt = times_t(qkvv[2 * heads + head, cut][:, :HD], do)
            dst = (pt * (dpt - delta)).astype(bf16)
            dvv[cut] += jnp.dot(pt.astype(bf16), do, preferred_element_type=f32)
            dkv[cut] += jnp.dot(dst, q, preferred_element_type=f32)
            dqt += jnp.dot(ktv[head, :, cut], dst, preferred_element_type=f32)
        dq = (dqt[:HD].T * shrink).astype(bf16)
        dqv[pl.ds(first, tile)] = dq
        qsend[head, which] = jnp.concatenate([dq[:rows], dq[rows:]], axis=1)
        send_gradient(0, head, which)

        @pl.when(step == TURNS - 1)
        def _():
            @pl.loop(0, 4)
            def _(at):
                there = lax.rem(group + 1 + at, 4)
                cut = pl.ds(pl.multiple_of(there * tile, tile), tile)
                pair = jnp.concatenate([dkv[cut] * shrink, dvv[cut]], axis=1).astype(bf16)
                kvsend[head, there] = pair
                send_gradient(1, head, there)
                dqkv[head, cut] = jnp.concatenate([pair, dqv[cut]], axis=1)

        @pl.when(turn == TURNS)
        def _():
            loads[4].wait()
            pass_small(0)

        for at in range(1, 4):
            pl.when(turn == TURNS + at)(functools.partial(pass_small, at))


    loads[5].wait()
    for head in range(heads - 1):
        absorb(head)
        product = times_t(joined[...], wv[head])
        xacc[...] = product if head == 0 else xacc[...] + product
    tick(heads * TURNS)
    absorb(heads - 1)
    loads[6].wait()
    for side in range(2):
        at = pl.ds(side * rows, rows)
        total = prev[at] + xacc[at] + times_t(joined[at], wv[heads - 1])
        xsend[side] = total.astype(bf16)
    return_rows(xsend, tgrad_ref, xsend_sem, xrecv_sem, "start")

    for head in range(heads):
        make_slab(head)
        tick(heads * TURNS + 1 + head)
    for head in range(heads):
        pass_slab(head)
    for now in range(heads * TURNS + 1 + heads, PHASE[-1][1] + UNITS):
        tick(now)

    def slabs_in(head, at):
        return [unfold(line_in[head, half_at * GROUPS + at].astype(f32)) for half_at in range(2)]

    for head in range(heads):
        for step in range(1, 8):
            there = lax.rem(blk + step, 8)
            landed(line_in.at[head, there], lrecv_sem.at[head, there])
    total = small_sum[3]
    own = [
        functools.reduce(jnp.add, slabs_in(at % heads, at // heads))
        for at in range(GROUPS * heads)
    ]
    each = width // 32
    bias = []
    for part in range(3):
        cut = slice((part + 2) % 3 * HD, (part + 2) % 3 * HD + HD)
        for pair in range(GROUPS * heads // 2):
            both_heads = jnp.concatenate([own[2 * pair][:, cut], own[2 * pair + 1][:, cut]], axis=1)
            lanes = slice(part * width + pair * LANES, part * width + (pair + 1) * LANES)
            wqkv_ref[:, lanes] = both_heads[:each]
            bias.append(both_heads[each:])
    pairs = GROUPS * heads // 2
    bias_q = jnp.concatenate(bias[:pairs], axis=1)
    bias_v = jnp.concatenate(bias[2 * pairs :], axis=1)
    bias = jnp.where(tab < 2, bias_q, bias_v)

    row = lax.broadcasted_iota(jnp.int32, (width, LANES), 0)
    lane = lax.broadcasted_iota(jnp.int32, (width, LANES), 1)

    def take(block, first, count):
        chosen = jnp.where((row == first + lane) & (lane < count), 1.0, 0.0)
        return jnp.dot(
            block, chosen, preferred_element_type=f32, precision=lax.Precision.HIGHEST
        )

    index = 8 * tab + blk
    little_ref[0:8] = take(total[:8], each * index, each)
    at_row = lax.broadcasted_iota(jnp.int32, total.shape, 0) == 6 + tab
    wide = jnp.sum(jnp.where(at_row, total, 0.0), axis=0, keepdims=True)
    little_ref[6:7] = take(jnp.broadcast_to(wide, (8, width)), 4 * each * blk, 4 * each)[:1]
    little_ref[7:8] = take(bias, 2 * each * lax.rem(index, 16), 2 * each)[:1]

    return_rows(xsend, tgrad_ref, xsend_sem, xrecv_sem, "wait")
    for step in range(1, 4):
        context_copy(group_at(step)).wait_send()

    @pl.loop(0, heads)
    def _(head):
        @pl.loop(1, 4)
        def _(step):
            for copy in gradient_copies(head, lax.rem(group + step, 4), False):
                copy.wait_send()

    for step in range(1, 8):
        for head in range(heads):
            slab_blk(head, step).wait_send()
    for at in range(3):
        small_pair(at).wait_send()
    for step in range(1, 4):
        small_tab(step).wait_send()
        for head in range(heads):
            slab_tab(head, step).wait_send()
            sums_tab(head, step).wait_send()

    stage_copy(0, UNITS - 1).wait_send()

    @pl.loop(0, UNITS)
    def _(unit):
        both(lambda order: stage_copy(1, unit, order).wait_send())
        both(lambda order: stage_copy(2, unit, order).wait_send())
        stage_copy(3, unit).wait_send()
        stage_copy(4, unit).wait_send()


def attend_back(dctx, qkv, ot, lse, full_t, by_head, pre, small, sums, parts, heads):
    width, total = full_t.shape
    blocks = 8
    rows = total // blocks
    each, ff = width // 32, 4 * width
    any_space = pl.BlockSpec(memory_space=pl.ANY)
    vmem = pl.BlockSpec(memory_space=pltpu.VMEM)
    bf16, f32 = jnp.bfloat16, jnp.float32
    dma = pltpu.SemaphoreType.DMA
    unit = parts.shape[-2:]
    shape = jax.ShapeDtypeStruct
    return pl.pallas_call(
        functools.partial(attend_back_kernel, heads),
        name="attend_back",
        out_shape=(
            shape((2, rows, width), bf16),
            shape((each, 3 * width), f32),
            shape((each, width), f32),
            shape((each, ff), f32),
            shape((4 * each, width), f32),
            shape((8, LANES), f32),
        ),
        in_specs=[any_space] * 9 + [vmem],
        out_specs=(any_space,) + (vmem,) * 5,
        scratch_shapes=[
            pltpu.VMEM((GROUPS, rows, 2 * heads * HD), bf16),
            pltpu.VMEM((heads, total, HD), bf16),
            pltpu.VMEM((heads, 4, 8, 2 * rows), f32),
            pltpu.VMEM((3 * heads, total, LANES), bf16),
            pltpu.VMEM(ot.shape, f32),
            pltpu.VMEM(lse.shape, f32),
            pltpu.VMEM((width, total), bf16),
            pltpu.VMEM(by_head.shape, bf16),
            pltpu.VMEM((2 * rows, width), f32),
            pltpu.VMEM((heads, LANES, total), bf16),
            pltpu.VMEM((total, HD), bf16),
            pltpu.VMEM((total, HD), f32),
            pltpu.VMEM((total, HD), f32),
            pltpu.VMEM((heads, total, 3 * HD), bf16),
            pltpu.VMEM((heads, 4, rows, 2 * HD), bf16),
            pltpu.VMEM((heads, 4, 2 * rows, 2 * HD), bf16),
            pltpu.VMEM((GROUPS * heads, rows, 2 * HD), bf16),
            pltpu.VMEM((GROUPS * heads, 2 * rows, 2 * HD), bf16),
            pltpu.VMEM((2 * rows, width), bf16),
            pltpu.VMEM((2 * rows, width), f32),
            pltpu.VMEM((2, rows, width), bf16),
            pltpu.VMEM((2, 2, 2, 2, *unit), bf16),
            pltpu.VMEM((UNITS, 2, 2, 2, 2, *unit), bf16),
            pltpu.VMEM((UNITS, 2, 2, 2, *unit), bf16),
            pltpu.VMEM((UNITS, 2, 2, *unit), bf16),
            pltpu.VMEM((UNITS, 2, *unit), bf16),
            pltpu.VMEM((UNITS, *unit), bf16),
            pltpu.VMEM((heads, 4, 6, 2 * each, 2 * HD), bf16),
            pltpu.VMEM((heads, 4, 6, 2 * each, 2 * HD), bf16),
            pltpu.VMEM((heads, 8, 3 * HD), f32),
            pltpu.VMEM((heads, 4, 8, 3 * HD), f32),
            pltpu.VMEM((heads, 8, (each + 8) // 2, 6 * HD), bf16),
            pltpu.VMEM((heads, 8, (each + 8) // 2, 6 * HD), bf16),
            pltpu.VMEM((4, 16, width), f32),
            pltpu.VMEM((4, 16, width), f32),
            pltpu.VMEM((3, 16, width), f32),
            dma((GROUPS,)),
            dma((GROUPS,)),
            dma((2, heads, 4)),
            dma((2, GROUPS * heads)),
            dma((2,)),
            dma((2,)),
            dma((STAGES, UNITS)),
            dma((STAGES, UNITS)),
            dma((2 * heads + 1, 4)),
            dma((2 * heads + 1, 4)),
            dma((heads + 1, 8)),
            dma((heads + 1, 8)),
            dma((8,)),
            dma((1,)),
        ],
        compiler_params=pltpu.CompilerParams(
            collective_id=2, has_side_effects=True, vmem_limit_bytes=62 << 20
        ),
    )(dctx, qkv, ot, lse, full_t, by_head, pre, sums, parts, small)


def finish_kernel(whole, *refs):
    little_ref, outs = refs[whole], refs[whole + 1 :]
    for src, dst in zip(refs[:whole], outs[:whole]):
        dst[...] = src[...]
    for at, dst in enumerate(outs[whole:]):
        dst[...] = little_ref[at, : dst.shape[0]]


def finish(arrays, little, counts):
    vmem = pl.BlockSpec(memory_space=pltpu.VMEM)
    shapes = [jax.ShapeDtypeStruct(a.shape, a.dtype) for a in arrays]
    shapes += [jax.ShapeDtypeStruct((count,), jnp.float32) for count in counts]
    return pl.pallas_call(
        functools.partial(finish_kernel, len(arrays)),
        name="finish",
        out_shape=tuple(shapes),
        in_specs=[vmem] * (len(arrays) + 1),
        out_specs=(vmem,) * len(shapes),
    )(*arrays, little)


def halves(grad):
    cut = grad.shape[2] // 2
    return jnp.concatenate([grad[:, :, :cut], grad[:, :, cut:]], axis=1)


def norm_parts(inputs):
    centred = inputs - jnp.mean(inputs, axis=-1, keepdims=True)
    inverse = lax.rsqrt(jnp.mean(centred * centred, axis=-1, keepdims=True) + EPSILON)
    return centred * inverse, inverse


def norm_back(grad, normed, inverse, gain):
    e = grad * gain
    return inverse * (
        e
        - jnp.mean(e, axis=-1, keepdims=True)
        - normed * jnp.mean(e * normed, axis=-1, keepdims=True)
    )


def column_sum(block):
    return jnp.sum(block.astype(jnp.float32), axis=0, keepdims=True)


def ffn_kernel(
    tok_ref,
    ctx_ref,
    cot_ref,
    par_ref,
    outw_ref,
    upw_hbm,
    downw_hbm,
    layer_ref,
    dctx_ref,
    pre_ref,
    small_ref,
    sums_ref,
    parts_ref,
    upw,
    downw,
    hid,
    hlow,
    hlow_t,
    norm1,
    slopes,
    active_t,
    pre2,
    gbranch,
    ghid,
    out,
    dparts,
    uparts,
    sum0,
    load_sem,
    keep_sem,
    osend_sem,
    orecv_sem,
    ssend_sem,
    srecv_sem,
):
    f32, bf16 = jnp.float32, jnp.bfloat16
    groups, rows, cols = ctx_ref.shape
    cols = cols // 2
    sides = 2
    width = tok_ref.shape[1]
    chunks = active_t.shape[0]
    each = width // 32
    tab, blk, chip, core = place()
    loads = (
        pltpu.make_async_copy(upw_hbm, upw, load_sem.at[0]),
        pltpu.make_async_copy(downw_hbm, downw, load_sem.at[1]),
    )
    for copy in loads:
        copy.start()

    greet_all(tab, blk)

    def par(at):
        return par_ref[at : at + 1]

    inverse1 = []
    contexts = [unfold(ctx_ref[group]) for group in range(groups)]
    for table in range(sides):
        cut = pl.ds(table * rows, rows)
        pre1 = tok_ref[cut].astype(f32) + par(0)
        for group in range(groups):
            pre1 += jnp.dot(
                contexts[group][table * rows : (table + 1) * rows],
                outw_ref[group * cols : (group + 1) * cols],
                preferred_element_type=f32,
            )
        normed, inverse = norm_parts(pre1)
        inverse1.append(inverse)
        hidden = normed * par(1) + par(2)
        low = hidden.astype(bf16)
        norm1[cut] = normed
        hid[cut] = hidden
        hlow[cut] = low
        hlow_t[:, cut] = low.T

    pre2[...] = hid[...] + par(3)
    for copy in loads:
        copy.wait()

    def forward(at):
        cut = pl.ds(pl.multiple_of(at * width, width), width)
        upper = jnp.dot(
            hlow[...], upw[:, cut], preferred_element_type=f32
        ) + par_ref[pl.ds(24 + at, 1)]
        cdf = 0.5 + 0.5 * lax.erf(upper * math.sqrt(0.5))
        act = (upper * cdf).astype(bf16)
        slopes[at] = cdf + upper * jnp.exp(-0.5 * upper * upper) * (1 / math.sqrt(2 * math.pi))
        active_t[at] = act.T
        pre2[...] += jnp.dot(act, downw[cut], preferred_element_type=f32)

    @pl.loop(0, chunks // 2)
    def _(pair):
        forward(2 * pair)
        forward(2 * pair + 1)

    normed, inverse = norm_parts(pre2[...])
    out[...] = (normed * par(4) + par(5)).astype(bf16).reshape(out.shape)
    return_rows(out, layer_ref, osend_sem, orecv_sem, "start")
    grad = cot_ref[...].astype(f32)
    small_ref[4:5] = column_sum(grad * normed)
    small_ref[5:6] = column_sum(grad)
    gpre2 = norm_back(grad, normed, inverse, par(4))
    ghid[...] = gpre2
    low = gpre2.astype(bf16)
    gbranch[...] = low
    small_ref[3:4] = column_sum(low)

    def core_copy(unit, src):
        return send_to(
            src.at[:, :, :, :, 1 - core],
            sum0.at[unit],
            ssend_sem.at[unit],
            srecv_sem.at[unit],
            (tab, 2 * chip + 1 - core),
        )

    def add_core(unit, parts):
        landed(sum0.at[unit], srecv_sem.at[unit])
        for a in range(2):
            for b in range(2):
                sum0[unit, a, b] = sum0[unit, a, b] + parts[a, b, :, :, core]

    @pl.loop(0, chunks)
    def _(at):
        wdown = jnp.dot(active_t[at], gbranch[...], preferred_element_type=f32)
        wdown = wdown.reshape(8, 4, each, width)
        for part in range(4):
            dparts[part, at // 2, lax.rem(at, 2)] = (
                halves(wdown[:, part]).astype(bf16).reshape(dparts.shape[3:])
            )

    for unit in range(4):
        core_copy(unit, dparts.at[unit]).start()

    @pl.loop(0, chunks)
    def _(at):
        cut = pl.ds(pl.multiple_of(at * width, width), width)

        @pl.when(jnp.logical_or(at == 1, at == 2))
        def _():
            for unit in (2 * at - 2, 2 * at - 1):
                add_core(unit, dparts.at[unit])

        gact = times_t(gbranch[...], downw[cut])
        gup = (gact * slopes[at]).astype(bf16)
        small_ref[pl.ds(6 + at, 1)] = column_sum(gup)
        ghid[...] += times_t(gup, upw[:, cut])
        wup = jnp.dot(hlow_t[...], gup, preferred_element_type=f32)
        uparts[at] = halves(wup.reshape(32, each, width)).astype(bf16).reshape(uparts.shape[1:])
        core_copy(4 + at, uparts.at[at]).start()

    small = [0.0, 0.0, 0.0]
    lows = []
    for table in range(sides):
        cut = pl.ds(table * rows, rows)
        grad, normed = ghid[cut], norm1[cut]
        small[1] += column_sum(grad * normed)
        small[2] += column_sum(grad)
        gpre1 = norm_back(grad, normed, inverse1[table], par(1))
        pre_ref[cut] = gpre1
        low = gpre1.astype(bf16)
        small[0] += column_sum(low)
        lows.append(low)
    low = jnp.concatenate(lows, axis=0)
    for at in range(3):
        small_ref[at : at + 1] = small[at]
    small_ref[10:] = jnp.zeros((6, width), f32)
    wouts = []
    for group in range(groups):
        dctx_ref[group] = fold(
            times_t(low, outw_ref[group * cols : (group + 1) * cols]).astype(bf16)
        )
        wout = jnp.dot(unfold(ctx_ref[group]).T, low, preferred_element_type=f32)
        wouts.append(halves(wout.reshape(8, each, width)).astype(bf16))
    for unit in range(4):
        core_copy(unit, dparts.at[unit]).wait_send()
    dparts[0] = jnp.concatenate(wouts, axis=0).reshape(dparts.shape[1:])
    keep = [pltpu.make_async_copy(dparts.at[0], parts_ref, keep_sem.at[0])]

    @pl.loop(0, 4)
    def _(at):
        add_core(4 + at, uparts.at[at])
        core_copy(4 + at, uparts.at[at]).wait_send()

    keep.append(pltpu.make_async_copy(sum0, sums_ref, keep_sem.at[1]))
    for copy in keep:
        copy.start()
    return_rows(out, layer_ref, osend_sem, orecv_sem, "wait")
    for copy in keep:
        copy.wait()


def ffn(tokens, ctx, cotangent, params, out_weight, up_weight, down_weight):
    total, width = tokens.shape
    chunks = up_weight.shape[1] // width
    unit = (2 * (width // 32), width // 2)
    any_space = pl.BlockSpec(memory_space=pl.ANY)
    vmem = pl.BlockSpec(memory_space=pltpu.VMEM)
    bf16, f32 = jnp.bfloat16, jnp.float32
    flops = 18 * total * width * chunks * width + 6 * total * width * width
    return pl.pallas_call(
        ffn_kernel,
        name="ffn",
        out_shape=(
            jax.ShapeDtypeStruct((2, total // 2, width), bf16),
            jax.ShapeDtypeStruct(ctx.shape, bf16),
            jax.ShapeDtypeStruct((total, width), f32),
            jax.ShapeDtypeStruct((16, width), f32),
            jax.ShapeDtypeStruct((8, 2, 2, 2, 2, *unit), bf16),
            jax.ShapeDtypeStruct((2, 2, 2, 2, 2, *unit), bf16),
        ),
        in_specs=[vmem, vmem, vmem, vmem, vmem, any_space, any_space],
        out_specs=(any_space, vmem, vmem, vmem, any_space, any_space),
        scratch_shapes=[
            pltpu.VMEM(up_weight.shape, bf16),
            pltpu.VMEM(down_weight.shape, bf16),
            pltpu.VMEM((total, width), f32),
            pltpu.VMEM((total, width), bf16),
            pltpu.VMEM((width, total), bf16),
            pltpu.VMEM((total, width), f32),
            pltpu.VMEM((chunks, total, width), f32),
            pltpu.VMEM((chunks, width, total), bf16),
            pltpu.VMEM((total, width), f32),
            pltpu.VMEM((total, width), bf16),
            pltpu.VMEM((total, width), f32),
            pltpu.VMEM((2, total // 2, width), bf16),
            pltpu.VMEM((4, 2, 2, 2, 2, 2, *unit), bf16),
            pltpu.VMEM((4, 2, 2, 2, 2, 2, *unit), bf16),
            pltpu.VMEM((8, 2, 2, 2, 2, *unit), bf16),
            pltpu.SemaphoreType.DMA((2,)),
            pltpu.SemaphoreType.DMA((2,)),
            pltpu.SemaphoreType.DMA((2,)),
            pltpu.SemaphoreType.DMA((2,)),
            pltpu.SemaphoreType.DMA((8,)),
            pltpu.SemaphoreType.DMA((8,)),
        ],
        compiler_params=pltpu.CompilerParams(
            collective_id=3, has_side_effects=True, vmem_limit_bytes=63 << 20
        ),
        cost_estimate=pl.CostEstimate(
            flops=flops, bytes_accessed=40 << 20, transcendentals=total * width * chunks
        ),
    )(tokens, ctx, cotangent, params, out_weight, up_weight, down_weight)


def shards_direct(
    tokens,
    lengths,
    qkv_weight,
    qkv_bias,
    out_weight,
    out_bias,
    attn_gain,
    attn_shift,
    up_weight,
    up_bias,
    down_weight,
    down_bias,
    ffn_gain,
    ffn_shift,
    cotangent,
):
    tables, rows, width = tokens.shape
    f32 = jnp.float32
    heads = width // HD // GROUPS
    row = lax.broadcasted_iota(jnp.int32, (32, width), 0)
    params = jnp.zeros((32, width), jnp.bfloat16)
    spans = [
        (at, at + 1, vector)
        for at, vector in enumerate(
            (out_bias, attn_gain, attn_shift, down_bias, ffn_gain, ffn_shift)
        )
    ]
    spans += [(8, 16, qkv_bias[:width]), (16, 24, qkv_bias[width:])]
    spans += [
        (24 + at, 25 + at, up_bias[at * width : (at + 1) * width])
        for at in range(up_bias.shape[0] // width)
    ]
    for first, last, vector in spans:
        params = jnp.where((row >= first) & (row < last), vector[None], params)

    params = params.astype(f32)
    ctx, my_tokens, my_cotangent, full_t, qkv, ot, lse, by_head = attend(
        tokens, lengths, params, qkv_weight, cotangent, heads
    )
    layer_out, dctx, pre, small, sums, parts = ffn(
        my_tokens.reshape(tables * rows, width),
        ctx,
        my_cotangent.reshape(tables * rows, width),
        params,
        out_weight,
        up_weight,
        down_weight,
    )
    *whole, little = attend_back(
        dctx, qkv, ot, lse, full_t, by_head, pre, small, sums, parts, heads
    )
    each = width // 32
    whole.insert(1, layer_out)
    (
        token_grad,
        layer_out,
        wgrad_qkv,
        wgrad_out,
        wgrad_up,
        wgrad_down,
        bgrad_out,
        ggrad_attn,
        sgrad_attn,
        bgrad_down,
        ggrad_ffn,
        sgrad_ffn,
        bgrad_up,
        bgrad_qkv,
    ) = finish(whole, little, [each] * 6 + [4 * each, 2 * each])
    return (
        layer_out,
        token_grad,
        wgrad_qkv,
        bgrad_qkv,
        wgrad_out,
        bgrad_out,
        ggrad_attn,
        sgrad_attn,
        wgrad_up,
        bgrad_up,
        wgrad_down,
        bgrad_down,
        ggrad_ffn,
        sgrad_ffn,
    )


def solution(mesh):
    in_specs = (
        P("tab", "blk", None),
        P("tab"),
        P(),
        P(),
        P(),
        P(),
        P(),
        P(),
        P(),
        P(),
        P(),
        P(),
        P(),
        P(),
        P("tab", "blk", None),
    )
    out_specs = (
        P("tab", "blk", None),
        P("tab", "blk", None),
        P(("tab", "blk"), None),
        P(("tab", "blk")),
        P(("tab", "blk"), None),
        P(("tab", "blk")),
        P(("tab", "blk")),
        P(("tab", "blk")),
        P(("tab", "blk"), None),
        P(("tab", "blk")),
        P(("tab", "blk"), None),
        P(("tab", "blk")),
        P(("tab", "blk")),
        P(("tab", "blk")),
    )
    tab_count, blk_count = mesh.shape["tab"], mesh.shape["blk"]

    def pick(*operands):
        table_count = operands[0].shape[0] // tab_count
        head_count = operands[0].shape[2] // HD
        direct = table_count == 2 and blk_count == 8 and tab_count == 4 and head_count % 4 == 0
        body = shards_direct if direct else shards_ring
        return jax.shard_map(
            body, mesh=mesh, in_specs=in_specs, out_specs=out_specs, check_vma=False
        )(*operands)

    return pick
```

profile of v0, /device:TPU:0, one launch (start us, length us, event | category | flops | bytes accessed | tf_op | source)
XLA Modules:
  0.0 195.3 jit_solution(15111227300179610413)
XLA Ops:
  0.7 0.8 fusion
  1.5 1.5 select_convert_fusion.par_ref
  3.0 57.7 %attend.1 = (bf16[4,256,384]{2,1,0:T(8,128)(2,1)}, bf16[2,256,768]{2,1,0:T(8,128)(2,1)}, bf16[2,256,768]{2,1,0:T(8,128)(2,1)}, bf16[768,2048]{1,0:T(8,128)(2,1)}...) custom-call(bf16[2,256,768]{2,1,0:T(8,128)(2,1)} %tok_ref.1, ...), custom_call_target="tpu_custom_call" | custom-call | tf_op jit(solution)/shard_map/attend/pallas_call | solution.py:744
  60.8 33.8 %ffn.1 = (bf16[2,256,768]{2,1,0:T(8,128)(2,1)}, bf16[4,256,384]{2,1,0:T(8,128)(2,1)}, f32[512,768]{1,0:T(8,128)}, f32[16,768]{1,0:T(8,128)}, bf16[8,2,2,2,2,48,3...) custom-call(bf16[512,768]{1,0:T(8,128)(2,1)} %bitcast.2, ...), custom_call_target="tpu_custom_call" | custom-call | flops 23555211264 | bytes 41943040 | tf_op jit(solution)/shard_map/ffn/pallas_call | solution.py:1652
  94.6 97.3 %attend_back.1 = (bf16[2,256,768]{2,1,0:T(8,128)(2,1)}, f32[24,2304]{1,0:T(8,128)}, f32[24,768]{1,0:T(8,128)}, f32[24,3072]{1,0:T(8,128)}, f32[96,768]{1,0:T(8,128)}, /*index=5*/f32[8,128]{1,0:T(8,128)}) custom-call(bf16[4,256,384]{2,1,0:T(8,128)(2,1)} %get-tuple-element.51.dctx_ref, bf16[9,2048,128]{2,1,0:T(8,128)(2,1)} %get-tuple-element.52.qkv_ref, ...), custom_call_target="tpu_custom_call" | custom-call | tf_op jit(solution)/shard_map/attend_back/pallas_call | solution.py:1335
  192.0 3.1 %finish.1 = (bf16[2,256,768]{2,1,0:T(8,128)(2,1)}, bf16[2,256,768]{2,1,0:T(8,128)(2,1)}, f32[24,2304]{1,0:T(8,128)}, f32[24,768]{1,0:T(8,128)}, f32[24,3072]{1,0...) custom-call(bf16[2,256,768]{2,1,0:T(8,128)(2,1)} %get-tuple-element., ...), custom_call_target="tpu_custom_call" | custom-call | tf_op jit(solution)/shard_map/finish/pallas_call | solution.py:1418
  (6 shorter events, 0.0 us)
where the time goes:
time: 196 us; the launch traced here: 195 us
  Pallas kernels  192 us (98%)
    pallas_call x1, Pallas kernels, attend_back(): pl.pallas_call(functools.partial(attend_back_kernel, heads), name='attend...  97.3 us
    pallas_call x1, Pallas kernels, attend(): pl.pallas_call(functools.partial(attend_kernel, heads), name='attend', ou...  57.7 us
    pallas_call x1, Pallas kernels, ffn(): pl.pallas_call(ffn_kernel, name='ffn', out_shape=(jax.ShapeDtypeStruct((2...  33.8 us

commit v1 on v0

--- a/solution.py
+++ b/solution.py
@@ -446,6 +446,7 @@
     ot_ref,
     lse_ref,
     wr_ref,
+    kt_ref,
     tokv,
     toktv,
     wfull,
@@ -454,10 +455,12 @@
     bown,
     qkvv,
     vtv,
+    ktv,
     otv,
     lsev,
     acc,
     peaks,
+    cotv,
     csend,
     send_sem,
     recv,
@@ -513,7 +516,8 @@
     pl.when(is_near)(to_other.start)
     to_mate.start()
     to_side.start()
-    tokv[blk] = tok_ref[half]
+    own_tokens = pltpu.make_async_copy(tok_ref.at[half], tokv.at[blk], local_sem.at[11])
+    own_tokens.start()
 
     lane1 = lax.broadcasted_iota(jnp.int32, (8, LANES), 1)
     for at in (0, 2):
@@ -550,6 +554,7 @@
             qkvv[heads + head, pl.ds(first, rows)] = (k + pad).astype(jnp.bfloat16)
             qkvv[2 * heads + head, pl.ds(first, rows)] = v.astype(jnp.bfloat16)
             vtv[head, :, pl.ds(first, rows)] = v.T.astype(jnp.bfloat16)
+            ktv[head, :, pl.ds(first, rows)] = k.T.astype(jnp.bfloat16)
         toktv[:, pl.ds(first, rows)] = tok.T
 
     def take_keys(tile, head, first_key, count, fresh):
@@ -583,7 +588,28 @@
             tile = jnp.where(at < heads, chip, jnp.where(at < 2 * heads, mate, other_near))
             take_keys(tile, lax.rem(at, heads), other_near * 2 * rows, 2 * rows, False)
 
+    def owner_of(table):
+        return 2 * table + chip // 2, lax.rem(chip, 2)
+
+    def cotangent_copy(table, own):
+        src, dst = cot_hbm.at[table], mycot_ref.at[core]
+        if own:
+            return pltpu.make_async_copy(cotv, dst, orecv_sem.at[core])
+        return remote(src, dst, osend_sem.at[table], orecv_sem.at[core], *owner_of(table))
+
+    def is_owner(table):
+        to_chip, to_core = owner_of(table)
+        return jnp.logical_and(to_chip == chip, to_core == core)
+
+    own_tokens.wait()
+    own_cotangent = pltpu.make_async_copy(cot_hbm.at[half], cotv, local_sem.at[10])
+    pl.when(is_owner(half))(own_cotangent.start)
     project(blk)
+
+    @pl.when(is_owner(half))
+    def _():
+        own_cotangent.wait()
+        cotangent_copy(half, True).start()
 
     def half_lanes(part, at):
         first = part * width + LANES * (at // 2)
@@ -620,19 +646,6 @@
         arrived(2 * src_chip + 1 - core)
         project(2 * src_chip + 1 - core)
 
-    def owner_of(table):
-        return 2 * table + chip // 2, lax.rem(chip, 2)
-
-    def cotangent_copy(table, own):
-        src, dst = cot_hbm.at[table], mycot_ref.at[core]
-        if own:
-            return pltpu.make_async_copy(src, dst, orecv_sem.at[core])
-        return remote(src, dst, osend_sem.at[table], orecv_sem.at[core], *owner_of(table))
-
-    def is_owner(table):
-        to_chip, to_core = owner_of(table)
-        return jnp.logical_and(to_chip == chip, to_core == core)
-
     pl.when(is_near)(functools.partial(pass_on, 1, other_near))
     meet_keys_of_own_half()
     pl.when(jnp.logical_not(is_near))(functools.partial(pass_on, 1, other_near))
@@ -647,11 +660,11 @@
         pltpu.make_async_copy(toktv, fullt_ref, local_sem.at[0]),
         pltpu.make_async_copy(qkvv, qkv_ref, local_sem.at[1]),
         pltpu.make_async_copy(wrv, wr_ref, local_sem.at[6]),
+        pltpu.make_async_copy(ktv, kt_ref, local_sem.at[9]),
     )
     for copy in keep:
         copy.start()
 
-    pl.when(is_owner(half))(cotangent_copy(half, True).start)
     pl.when(jnp.logical_not(is_owner(half)))(cotangent_copy(half, False).start)
     my_tokens = [
         pltpu.make_async_copy(
@@ -753,9 +766,16 @@
             jax.ShapeDtypeStruct((4, heads * HD, 2 * rows), f32),
             jax.ShapeDtypeStruct((4, 8, 2 * rows), f32),
             jax.ShapeDtypeStruct((heads, width, width), bf16),
+            jax.ShapeDtypeStruct((heads, LANES, total), bf16),
         ),
-        in_specs=[vmem, pl.BlockSpec(memory_space=pltpu.SMEM), vmem, any_space, any_space],
-        out_specs=(any_space,) * 8,
+        in_specs=[
+            any_space,
+            pl.BlockSpec(memory_space=pltpu.SMEM),
+            vmem,
+            any_space,
+            any_space,
+        ],
+        out_specs=(any_space,) * 9,
         scratch_shapes=[
             pltpu.VMEM((blocks, rows, width), bf16),
             pltpu.VMEM((width, total), bf16),
@@ -765,10 +785,12 @@
             pltpu.VMEM((8, 3 * heads * LANES), f32),
             pltpu.VMEM((3 * heads, total, LANES), bf16),
             pltpu.VMEM((heads, LANES, total), bf16),
+            pltpu.VMEM((heads, LANES, total), bf16),
             pltpu.VMEM((4, heads * HD, 2 * rows), f32),
             pltpu.VMEM((4, 8, 2 * rows), f32),
             pltpu.VMEM((4, heads, LANES, 2 * rows), f32),
             pltpu.VMEM((4, 8, 2 * rows), f32),
+            pltpu.VMEM((rows, width), bf16),
             pltpu.VMEM((GROUPS, rows, 2 * heads * HD), bf16),
             dma((8,)),
             dma((blocks,)),
@@ -776,7 +798,7 @@
             dma((GROUPS,)),
             dma((2,)),
             dma((2,)),
-            dma((9,)),
+            dma((12,)),
         ],
         compiler_params=pltpu.CompilerParams(
             collective_id=1, has_side_effects=True, vmem_limit_bytes=60 << 20
@@ -796,6 +818,7 @@
     qkv_ref,
     ot_ref,
     lse_ref,
+    kt_ref,
     fullt_ref,
     w_ref,
     pre_ref,
@@ -885,10 +908,11 @@
                 (w_ref, wv),
                 (pre_ref, prev),
                 (sums_ref, sum0.at[: UNITS - 1]),
+                (kt_ref, ktv),
             )
         )
     ]
-    for copy in [*loads[:4], loads[7]]:
+    for copy in [*loads[:4], loads[8], loads[7]]:
         copy.start()
 
     greet_all(tab, blk)
@@ -1103,10 +1127,8 @@
         for step in range(1, 8):
             slab_blk(head, step).start()
 
-    for copy in loads[:4]:
+    for copy in [*loads[:4], loads[8]]:
         copy.wait()
-    for head in range(heads):
-        ktv[head] = qkvv[heads + head].T
 
     def gradient_copies(head, which, own):
         slot = group * heads + head
@@ -1166,11 +1188,13 @@
                 landed(dov.at[which], drecv_sem.at[which])
 
             dos = unfold(dov[which])
+            dos_t = dos.T.astype(f32)
             for at in range(heads):
                 do = dos[:, at * HD : (at + 1) * HD]
                 doh[at, pl.ds(first, tile)] = do
-                ot = otv[which, at * HD : (at + 1) * HD]
-                deltas[at, which, :1] = jnp.sum(ot * do.astype(f32).T, axis=0, keepdims=True)
+                rows_at = slice(at * HD, (at + 1) * HD)
+                ot = otv[which, rows_at]
+                deltas[at, which, :1] = jnp.sum(ot * dos_t[rows_at], axis=0, keepdims=True)
 
         @pl.when(step == 0)
         def _():
@@ -1321,7 +1345,7 @@
         stage_copy(4, unit).wait_send()
 
 
-def attend_back(dctx, qkv, ot, lse, full_t, by_head, pre, small, sums, parts, heads):
+def attend_back(dctx, qkv, ot, lse, kt, full_t, by_head, pre, small, sums, parts, heads):
     width, total = full_t.shape
     blocks = 8
     rows = total // blocks
@@ -1343,7 +1367,7 @@
             shape((4 * each, width), f32),
             shape((8, LANES), f32),
         ),
-        in_specs=[any_space] * 9 + [vmem],
+        in_specs=[any_space] * 10 + [vmem],
         out_specs=(any_space,) + (vmem,) * 5,
         scratch_shapes=[
             pltpu.VMEM((GROUPS, rows, 2 * heads * HD), bf16),
@@ -1394,13 +1418,13 @@
             dma((2 * heads + 1, 4)),
             dma((heads + 1, 8)),
             dma((heads + 1, 8)),
-            dma((8,)),
+            dma((9,)),
             dma((1,)),
         ],
         compiler_params=pltpu.CompilerParams(
             collective_id=2, has_side_effects=True, vmem_limit_bytes=62 << 20
         ),
-    )(dctx, qkv, ot, lse, full_t, by_head, pre, sums, parts, small)
+    )(dctx, qkv, ot, lse, kt, full_t, by_head, pre, sums, parts, small)
 
 
 def finish_kernel(whole, *refs):
@@ -1449,11 +1473,11 @@
 
 
 def ffn_kernel(
-    tok_ref,
-    ctx_ref,
-    cot_ref,
+    tok_hbm,
+    ctx_hbm,
+    cot_hbm,
     par_ref,
-    outw_ref,
+    outw_hbm,
     upw_hbm,
     downw_hbm,
     layer_ref,
@@ -1462,6 +1486,10 @@
     small_ref,
     sums_ref,
     parts_ref,
+    tok_ref,
+    ctx_ref,
+    cot_ref,
+    outw_ref,
     upw,
     downw,
     hid,
@@ -1496,10 +1524,20 @@
         pltpu.make_async_copy(upw_hbm, upw, load_sem.at[0]),
         pltpu.make_async_copy(downw_hbm, downw, load_sem.at[1]),
     )
+    first = [
+        pltpu.make_async_copy(src, dst, load_sem.at[2 + at])
+        for at, (src, dst) in enumerate(
+            ((tok_hbm, tok_ref), (ctx_hbm, ctx_ref), (outw_hbm, outw_ref), (cot_hbm, cot_ref))
+        )
+    ]
+    for copy in first:
+        copy.start()
     for copy in loads:
         copy.start()
 
     greet_all(tab, blk)
+    for copy in first:
+        copy.wait()
 
     def par(at):
         return par_ref[at : at + 1]
@@ -1660,9 +1698,13 @@
             jax.ShapeDtypeStruct((8, 2, 2, 2, 2, *unit), bf16),
             jax.ShapeDtypeStruct((2, 2, 2, 2, 2, *unit), bf16),
         ),
-        in_specs=[vmem, vmem, vmem, vmem, vmem, any_space, any_space],
+        in_specs=[any_space] * 3 + [vmem] + [any_space] * 3,
         out_specs=(any_space, vmem, vmem, vmem, any_space, any_space),
         scratch_shapes=[
+            pltpu.VMEM(tokens.shape, bf16),
+            pltpu.VMEM(ctx.shape, bf16),
+            pltpu.VMEM(cotangent.shape, bf16),
+            pltpu.VMEM(out_weight.shape, bf16),
             pltpu.VMEM(up_weight.shape, bf16),
             pltpu.VMEM(down_weight.shape, bf16),
             pltpu.VMEM((total, width), f32),
@@ -1678,7 +1720,7 @@
             pltpu.VMEM((4, 2, 2, 2, 2, 2, *unit), bf16),
             pltpu.VMEM((4, 2, 2, 2, 2, 2, *unit), bf16),
             pltpu.VMEM((8, 2, 2, 2, 2, *unit), bf16),
-            pltpu.SemaphoreType.DMA((2,)),
+            pltpu.SemaphoreType.DMA((6,)),
             pltpu.SemaphoreType.DMA((2,)),
             pltpu.SemaphoreType.DMA((2,)),
             pltpu.SemaphoreType.DMA((2,)),
@@ -1731,7 +1773,7 @@
         params = jnp.where((row >= first) & (row < last), vector[None], params)
 
     params = params.astype(f32)
-    ctx, my_tokens, my_cotangent, full_t, qkv, ot, lse, by_head = attend(
+    ctx, my_tokens, my_cotangent, full_t, qkv, ot, lse, by_head, kt = attend(
         tokens, lengths, params, qkv_weight, cotangent, heads
     )
     layer_out, dctx, pre, small, sums, parts = ffn(
@@ -1744,7 +1786,7 @@
         down_weight,
     )
     *whole, little = attend_back(
-        dctx, qkv, ot, lse, full_t, by_head, pre, small, sums, parts, heads
+        dctx, qkv, ot, lse, kt, full_t, by_head, pre, small, sums, parts, heads
     )
     each = width // 32
     whole.insert(1, layer_out)

time: 196 us -> 195 us (level)
  no operation moved by 1% of the time
where the time goes in v1:
time: 195 us; the launch traced here: 194 us
  Pallas kernels  191 us (98%)
    pallas_call x1, Pallas kernels, attend_back(): pl.pallas_call(functools.partial(attend_back_kernel, heads), name='attend...  97.1 us
    pallas_call x1, Pallas kernels, attend(): pl.pallas_call(functools.partial(attend_kernel, heads), name='attend', ou...  57.8 us
    pallas_call x1, Pallas kernels, ffn(): pl.pallas_call(ffn_kernel, name='ffn', out_shape=(jax.ShapeDtypeStruct((2...  33 us

profile of v1, /device:TPU:0, one launch (start us, length us, event | category | flops | bytes accessed | tf_op | source)
XLA Modules:
  0.0 194.3 jit_solution(7913345607346459948)
XLA Ops:
  0.7 0.8 fusion
  1.5 1.5 select_convert_fusion.par_ref
  3.0 57.8 %attend.1 = (bf16[4,256,384]{2,1,0:T(8,128)(2,1)}, bf16[2,256,768]{2,1,0:T(8,128)(2,1)}, bf16[2,256,768]{2,1,0:T(8,128)(2,1)}, bf16[768,2048]{1,0:T(8,128)(2,1)}...) custom-call(bf16[2,256,768]{2,1,0:T(8,128)(2,1)} %tok_ref.1, ...), custom_call_target="tpu_custom_call" | custom-call | tf_op jit(solution)/shard_map/attend/pallas_call | solution.py:757
  60.9 33.0 %ffn.1 = (bf16[2,256,768]{2,1,0:T(8,128)(2,1)}, bf16[4,256,384]{2,1,0:T(8,128)(2,1)}, f32[512,768]{1,0:T(8,128)}, f32[16,768]{1,0:T(8,128)}, bf16[8,2,2,2,2,48,3...) custom-call(bf16[512,768]{1,0:T(8,128)(2,1)} %bitcast.2, ...), custom_call_target="tpu_custom_call" | custom-call | flops 23555211264 | bytes 41943040 | tf_op jit(solution)/shard_map/ffn/pallas_call | solution.py:1690
  93.9 97.1 %attend_back.1 = (bf16[2,256,768]{2,1,0:T(8,128)(2,1)}, f32[24,2304]{1,0:T(8,128)}, f32[24,768]{1,0:T(8,128)}, f32[24,3072]{1,0:T(8,128)}, f32[96,768]{1,0:T(8,128)}, /*index=5*/f32[8,128]{1,0:T(8,128)}) custom-call(bf16[4,256,384]{2,1,0:T(8,128)(2,1)} %get-tuple-element.52.dctx_ref, bf16[9,2048,128]{2,1,0:T(8,128)(2,1)} %get-tuple-element.53.qkv_ref, ...), custom_call_target="tpu_custom_call" | custom-call | tf_op jit(solution)/shard_map/attend_back/pallas_call | solution.py:1359
  191.0 3.1 %finish.1 = (bf16[2,256,768]{2,1,0:T(8,128)(2,1)}, bf16[2,256,768]{2,1,0:T(8,128)(2,1)}, f32[24,2304]{1,0:T(8,128)}, f32[24,768]{1,0:T(8,128)}, f32[24,3072]{1,0...) custom-call(bf16[2,256,768]{2,1,0:T(8,128)(2,1)} %get-tuple-element., ...), custom_call_target="tpu_custom_call" | custom-call | tf_op jit(solution)/shard_map/finish/pallas_call | solution.py:1442
  (6 shorter events, 0.0 us)

commit v2 on v1

--- a/solution.py
+++ b/solution.py
@@ -1638,6 +1638,9 @@
         uparts[at] = halves(wup.reshape(32, each, width)).astype(bf16).reshape(uparts.shape[1:])
         core_copy(4 + at, uparts.at[at]).start()
 
+    down_sums = pltpu.make_async_copy(sum0.at[:4], sums_ref.at[:4], keep_sem.at[2])
+    down_sums.start()
+
     small = [0.0, 0.0, 0.0]
     lows = []
     for table in range(sides):
@@ -1665,15 +1668,16 @@
         core_copy(unit, dparts.at[unit]).wait_send()
     dparts[0] = jnp.concatenate(wouts, axis=0).reshape(dparts.shape[1:])
     keep = [pltpu.make_async_copy(dparts.at[0], parts_ref, keep_sem.at[0])]
+    keep[0].start()
 
     @pl.loop(0, 4)
     def _(at):
         add_core(4 + at, uparts.at[at])
         core_copy(4 + at, uparts.at[at]).wait_send()
 
-    keep.append(pltpu.make_async_copy(sum0, sums_ref, keep_sem.at[1]))
-    for copy in keep:
-        copy.start()
+    keep.append(pltpu.make_async_copy(sum0.at[4:], sums_ref.at[4:], keep_sem.at[1]))
+    keep[1].start()
+    keep.append(down_sums)
     return_rows(out, layer_ref, osend_sem, orecv_sem, "wait")
     for copy in keep:
         copy.wait()
@@ -1721,7 +1725,7 @@
             pltpu.VMEM((4, 2, 2, 2, 2, 2, *unit), bf16),
             pltpu.VMEM((8, 2, 2, 2, 2, *unit), bf16),
             pltpu.SemaphoreType.DMA((6,)),
-            pltpu.SemaphoreType.DMA((2,)),
+            pltpu.SemaphoreType.DMA((3,)),
             pltpu.SemaphoreType.DMA((2,)),
             pltpu.SemaphoreType.DMA((2,)),
             pltpu.SemaphoreType.DMA((8,)),

time: 195 us -> 194 us (level)
  no operation moved by 1% of the time
where the time goes in v2:
time: 194 us; the launch traced here: 193 us
  Pallas kernels  190 us (98%)
    pallas_call x1, Pallas kernels, attend_back(): pl.pallas_call(functools.partial(attend_back_kernel, heads), name='attend...  97.1 us
    pallas_call x1, Pallas kernels, attend(): pl.pallas_call(functools.partial(attend_kernel, heads), name='attend', ou...  57.8 us
    pallas_call x1, Pallas kernels, ffn(): pl.pallas_call(ffn_kernel, name='ffn', out_shape=(jax.ShapeDtypeStruct((2...  32 us

profile of v2, /device:TPU:0, one launch (start us, length us, event | category | flops | bytes accessed | tf_op | source)
XLA Modules:
  0.0 193.3 jit_solution(12472137201199931862)
XLA Ops:
  0.7 0.8 fusion
  1.5 1.5 select_convert_fusion.par_ref
  3.0 57.8 %attend.1 = (bf16[4,256,384]{2,1,0:T(8,128)(2,1)}, bf16[2,256,768]{2,1,0:T(8,128)(2,1)}, bf16[2,256,768]{2,1,0:T(8,128)(2,1)}, bf16[768,2048]{1,0:T(8,128)(2,1)}...) custom-call(bf16[2,256,768]{2,1,0:T(8,128)(2,1)} %tok_ref.1, ...), custom_call_target="tpu_custom_call" | custom-call | tf_op jit(solution)/shard_map/attend/pallas_call | solution.py:757
  60.9 32.0 %ffn.1 = (bf16[2,256,768]{2,1,0:T(8,128)(2,1)}, bf16[4,256,384]{2,1,0:T(8,128)(2,1)}, f32[512,768]{1,0:T(8,128)}, f32[16,768]{1,0:T(8,128)}, bf16[8,2,2,2,2,48,3...) custom-call(bf16[512,768]{1,0:T(8,128)(2,1)} %bitcast.2, ...), custom_call_target="tpu_custom_call" | custom-call | flops 23555211264 | bytes 41943040 | tf_op jit(solution)/shard_map/ffn/pallas_call | solution.py:1694
  92.8 97.1 %attend_back.1 = (bf16[2,256,768]{2,1,0:T(8,128)(2,1)}, f32[24,2304]{1,0:T(8,128)}, f32[24,768]{1,0:T(8,128)}, f32[24,3072]{1,0:T(8,128)}, f32[96,768]{1,0:T(8,128)}, /*index=5*/f32[8,128]{1,0:T(8,128)}) custom-call(bf16[4,256,384]{2,1,0:T(8,128)(2,1)} %get-tuple-element.52.dctx_ref, bf16[9,2048,128]{2,1,0:T(8,128)(2,1)} %get-tuple-element.53.qkv_ref, ...), custom_call_target="tpu_custom_call" | custom-call | tf_op jit(solution)/shard_map/attend_back/pallas_call | solution.py:1359
  190.0 3.1 %finish.1 = (bf16[2,256,768]{2,1,0:T(8,128)(2,1)}, bf16[2,256,768]{2,1,0:T(8,128)(2,1)}, f32[24,2304]{1,0:T(8,128)}, f32[24,768]{1,0:T(8,128)}, f32[24,3072]{1,0...) custom-call(bf16[2,256,768]{2,1,0:T(8,128)(2,1)} %get-tuple-element., ...), custom_call_target="tpu_custom_call" | custom-call | tf_op jit(solution)/shard_map/finish/pallas_call | solution.py:1442
  (6 shorter events, 0.0 us)
